TPU v7x, 256 devices: a whole 4x4x8 slice. The times are simulated.
256 devices in a mesh: row: 16 (over z, core), col: 4 (over x), depth: 4 (over y).
Axes of the slice: x: 4, y: 4, z: 8, core: 2. Of those that a mesh axis runs over, the one named last changes fastest.
Arguments:
- residual: float32 [2048, 4096], P(('row', 'depth'), 'col'), may hold values from -4 to 4
- amplitudes: float32 [2048, 65536], P('col', ('row', 'depth')), may hold values from -6 to 6
- integrals: float32 [65536, 4096], P(('row', 'depth'), 'col'), may hold values from -0.0390625 to 0.0390625
- t2_mask: int32 [16, 512], P('col', ('row', 'depth')), may hold values from 0 to 1, as said below
- v_mask: int32 [512, 32], P(('row', 'depth'), 'col'), may hold values from 0 to 1, as said below
Outputs:
- updated: float32 [2048, 4096], P(('row', 'depth'), 'col')
Inputs may be any that keep to these rules, and one draw needn't show every extreme that they name: `t2_mask`: each entry flags one 128 x 128 amplitude tile as kept (1) or zero (0). `v_mask`: each entry flags one 128 x 128 integral tile as kept (1) or zero (0).
All inputs are finite; a program needn't handle non-finite values.
Results may differ from a plain program's by a relative error of at most 0.0001.
Values sent between devices are 32-bit elements; how exact they have to be, the bound alone decides.
A program may use at most 64 MiB of HBM per device.

v0:
```python
import jax
import jax.numpy as jnp
from jax import lax
from jax.sharding import PartitionSpec as P

TILE = 128


def apply_flags(matrix, tile_flags):
    tile_rows, tile_cols = tile_flags.shape
    tiled = (
        matrix.reshape(tile_rows, TILE, tile_cols, TILE)
        * tile_flags.astype(jnp.float32)[:, None, :, None]
    )
    return tiled.reshape(matrix.shape)


def per_device(residual, amplitudes, integrals, t2_mask, v_mask):
    amplitude_kept = apply_flags(amplitudes, t2_mask)
    integral_kept = apply_flags(integrals, v_mask)
    panels = lax.all_gather(amplitude_kept, "col", axis=0, tiled=True)
    summed = lax.psum_scatter(
        jnp.dot(
            panels,
            integral_kept,
            precision=lax.Precision.HIGHEST,
            preferred_element_type=jnp.float32,
        ),
        ("row", "depth"),
        scatter_dimension=0,
        tiled=True,
    )
    return residual + summed


def solution(mesh):
    in_specs = (
        P(("row", "depth"), "col"),
        P("col", ("row", "depth")),
        P(("row", "depth"), "col"),
        P("col", ("row", "depth")),
        P(("row", "depth"), "col"),
    )
    out_specs = P(("row", "depth"), "col")
    return jax.shard_map(
        per_device, mesh=mesh, in_specs=in_specs, out_specs=out_specs, check_vma=False
    )
```

profile of v0, /device:TPU:4, one launch (start us, length us, event | category | flops | bytes accessed | tf_op | source)
XLA Modules:
  0.0 295.0 jit_solution(5104896567255951643)
XLA Ops:
  6.5 0.0 all-gather.2.cloned.1.call-start
  6.5 0.7 convert_element_type.6
  7.2 0.2 mul.22
  7.4 0.0 copy-start.1
  7.4 3.7 %bitcast_multiply_fusion.2 = f32[512,1024]{1,0:T(8,128)} fusion(f32[512,1024]{1,0:T(8,128)} %param.6, f32[64,8,8,128]{3,2,1,0:T(8,128)S(1)} %bitcast.10), kind=kLoop, calls=%fused_computation.3 | loop fusion | flops 524288 | bytes 6291456 | tf_op jit(solution)/shard_map/mul | solution.py:12
  11.1 0.0 all-gather.2.cloned.1.call-update
  11.1 0.0 reduce-scatter.2.cloned.1.call-start
  11.2 0.0 copy-done.1
  11.2 88.4 %all-gather.2.cloned.1.call-done = f32[2048,1024]{1,0:T(8,128)} async-done(((f32[512,1024]{1,0:T(8,128)}), f32[2048,1024]{1,0:T(8,128)}) %all-gather.2.cloned.1.call-update) | async-done | bytes 8388624 | tf_op jit(solution)/shard_map/all_gather | solution.py:21
  99.6 0.0 copy-start.2
  99.6 0.3 mul.25
  99.9 1.8 copy-done.2
  101.8 32.0 %fusion = f32[2048,1024]{1,0:T(8,128)} fusion(f32[2048,1024]{1,0:T(8,128)} %all-gather.2.cloned.1.call-done, f32[1024,1024]{1,0:T(8,128)S(1)} %copy-done.2, f32[128,8,8,128]{3,2,1,0:T(8,128)S(1)} %bitcast.11), kind=kOutput, calls=%fused_computation.1 | convolution fusion | flops 25770852352 | bytes 25165824 | tf_op jit(solution)/shard_map/dot_general | solution.py:23
  133.7 0.0 copy-start
  133.7 0.0 reduce-scatter.2.cloned.1.call-update
  133.8 152.9 %reduce-scatter.2.cloned.1.call-done = f32[32,1024]{1,0:T(8,128)} async-done(((f32[2048,1024]{1,0:T(8,128)}), f32[32,1024]{1,0:T(8,128)}) %reduce-scatter.2.cloned.1.call-update) | async-done | bytes 131088 | tf_op jit(solution)/shard_map/reduce_scatter | solution.py:22
  286.6 0.0 copy-done
  286.6 1.6 add.5
  (1 shorter events, 0.0 us)
Async XLA Ops:
  6.5 93.0 %all-gather.2.cloned.1.call-start = ((), (), s32[]{:S(2)}) async-start(), calls=%async_computation.1 | async-start | bytes 10485760 | tf_op jit(solution)/shard_map/all_gather | solution.py:21
  7.4 3.8 %copy-start.1 = (s32[8,8]{1,0:T(8,128)S(1)}, s32[8,8]{1,0:T(8,128)}, u32[]{:S(2)}) copy-start(s32[8,8]{1,0:T(8,128)} %param.9) | copy-start | bytes 772
  11.1 275.5 %reduce-scatter.2.cloned.1.call-start = ((), (), s32[]{:S(2)}) async-start(), calls=%async_computation.2 | async-start | bytes 8519680 | tf_op jit(solution)/shard_map/reduce_scatter | solution.py:22
  99.6 2.2 copy-start.2
  133.7 152.9 %copy-start = (f32[32,1024]{1,0:T(8,128)S(1)}, f32[32,1024]{1,0:T(8,128)}, u32[]{:S(2)}) copy-start(f32[32,1024]{1,0:T(8,128)} %param.5) | copy-start | bytes 393220
Sparse Core Ops, SparseCore 0:
  11.3 88.2 all-gather.1
  133.9 152.6 reduce-scatter.1
where the time goes:
time: 295 us
  waiting for transfers between devices  241 us (82%)
  matrix products  32 us (11%)
  between operations  13.4 us (5%)
  other arithmetic  5.93 us (2%)
    reduce_scatter x1, waiting for transfers between devices, per_device(): lax.psum_scatter(jnp.dot(panels, integral_kept, precision=lax.Precision.H...  153 us
    all_gather x1, waiting for transfers between devices, per_device(): panels = lax.all_gather(amplitude_kept, 'col', axis=0, tiled=True)  88.4 us
    dot_general x1, matrix products, per_device(): jnp.dot(panels, integral_kept, precision=lax.Precision.HIGHEST, preferred...  32 us
  transfers between devices with their start and end apart: 2, of which 2 were waited for; matrix products, arithmetic and copies ran while one was open for 0% of the time, Pallas kernels for 0%

commit v1 on v0

v1 whole, which is shorter than its diff:
```python
import jax
import jax.numpy as jnp
from jax import lax
from jax.experimental import pallas as pl
from jax.experimental.pallas import tpu as pltpu
from jax.sharding import PartitionSpec as P

TILE = 128
NX, NY, NZ = 4, 4, 8
SUB = 8
NH = 32 // SUB
STEPS = 4 * NH
CD = 1024
AB = 1024
HALF = AB // 2
MESH = pl.DeviceIdType.MESH


def expand_lanes(flags):
    values = flags.astype(jnp.float32)
    return jnp.concatenate(
        [jnp.broadcast_to(values[:, q : q + 1], (values.shape[0], TILE)) for q in range(8)],
        axis=1,
    )


def kernel(
    amp, integ, t2_mask, v_mask, out,
    a_all, v_f32, v_hi, v_lo, a_hl, part, c_in, s_sum, y1_in, y2_out, y2_in, r_out, r_own, z_in,
    t2_all, v_flags, a_flags,
    a_send, a_recv, own_sem, v_sem, m_send, m_recv, m_sem,
    c_send, c_recv, y1_send, y1_recv, y2_send, y2_recv, z_send, z_recv,
):
    row = lax.axis_index("row")
    x = lax.axis_index("col")
    y = lax.axis_index("depth")
    z = row // 2
    core = row % 2
    right, left = (x + 1) % NX, (x + 3) % NX
    up, down, far = (y + 1) % NY, (y + 3) % NY, (y + 2) % NY
    sibling = z * 2 + 1 - core

    def own_copy(h, zz):
        return pltpu.make_async_copy(
            amp.at[zz, :, :, pl.ds(h * SUB, SUB), :], a_all.at[h, zz], own_sem.at[h, zz]
        )

    def v_copy(q):
        block = pl.ds(q * TILE, TILE)
        return pltpu.make_async_copy(integ.at[block, :], v_f32.at[block, :], v_sem.at[q])

    m_copy = pltpu.make_async_copy(t2_mask, t2_all.at[x], m_sem.at[0])
    vm_copy = pltpu.make_async_copy(v_mask, v_flags, m_sem.at[1])
    m_copy.start()
    vm_copy.start()
    for q in range(8):
        v_copy(q).start()
    for h in range(NH):
        own_copy(h, 0).start()
        own_copy(h, 1).start()

    barrier = pltpu.get_barrier_semaphore()

    def greet(r, c, d):
        pl.semaphore_signal(barrier, inc=1, device_id=(r, c, d), device_id_type=MESH)

    for k in range(1, NX):
        greet(row, (x + k) % NX, y)
    greet(sibling, x, y)
    greet(row, x, up)
    greet(row, x, down)
    for k in range(1, NZ):
        greet(((z + k) % NZ) * 2 + core, x, y)
    pl.semaphore_wait(barrier, NX - 1 + 3 + NZ - 1)

    def a_own_send(j, side):
        zz = (side + j // NH) % 2
        return pltpu.make_async_remote_copy(
            src_ref=amp.at[zz, :, :, pl.ds((j % NH) * SUB, SUB), :],
            dst_ref=a_all.at[NH + j, side],
            send_sem=a_send.at[side, j],
            recv_sem=a_recv.at[side, j],
            device_id=(row, right if side == 0 else left, y),
            device_id_type=MESH,
        )

    def a_forward(j, side):
        return pltpu.make_async_remote_copy(
            src_ref=a_all.at[NH + j, side],
            dst_ref=a_all.at[3 * NH + j, side],
            send_sem=a_send.at[side, 2 * NH + j],
            recv_sem=a_recv.at[side, 2 * NH + j],
            device_id=(row, right if side == 0 else left, y),
            device_id_type=MESH,
        )

    def flag_send(k):
        return pltpu.make_async_remote_copy(
            src_ref=t2_mask,
            dst_ref=t2_all.at[x],
            send_sem=m_send.at[k - 1],
            recv_sem=m_recv.at[k - 1],
            device_id=(row, (x + k) % NX, y),
            device_id_type=MESH,
        )

    for k in range(1, NX):
        flag_send(k).start()
    for j in range(2 * NH):
        a_own_send(j, 0).start()
        a_own_send(j, 1).start()

    vm_copy.wait()
    flags_v = expand_lanes(v_flags[...])
    for q in range(8):
        v_copy(q).wait()
        rows = slice(q * TILE, (q + 1) * TILE)
        kept = v_f32[rows, :] * flags_v[q : q + 1, :]
        hi = kept.astype(jnp.bfloat16)
        v_hi[rows, :] = hi
        v_lo[rows, :] = (kept - hi.astype(jnp.float32)).astype(jnp.bfloat16)

    m_copy.wait()
    for k in range(1, NX):
        flag_send(k).wait()
    for s in range(NX):
        wide = expand_lanes(t2_all[s])
        for p in range(4):
            a_flags[s * 4 + p] = wide[p : p + 1, :]

    def piece(i, side):
        group = i // NH
        away = (group + 1) // 2
        late = (group // 2) * (1 - group % 2)
        if side == 0:
            return (x + NX - away) % NX, late
        return (x + away) % NX, 1 - late

    def c_copy(i):
        return pltpu.make_async_remote_copy(
            src_ref=part.at[i, :, 1 - core],
            dst_ref=c_in.at[i],
            send_sem=c_send.at[i],
            recv_sem=c_recv.at[i],
            device_id=(sibling, x, y),
            device_id_type=MESH,
        )

    def y1_copy(i, side):
        return pltpu.make_async_remote_copy(
            src_ref=s_sum.at[i, :, far, :, pl.ds(side * HALF, HALF)],
            dst_ref=y1_in.at[i, side],
            send_sem=y1_send.at[side, i],
            recv_sem=y1_recv.at[side, i],
            device_id=(row, x, up if side == 0 else down),
            device_id_type=MESH,
        )

    def y2_copy(i, side):
        return pltpu.make_async_remote_copy(
            src_ref=y2_out.at[i, side],
            dst_ref=y2_in.at[i, side],
            send_sem=y2_send.at[side, i],
            recv_sem=y2_recv.at[side, i],
            device_id=(row, x, up if side == 0 else down),
            device_id_type=MESH,
        )

    def z_copy(i, side, target):
        return pltpu.make_async_remote_copy(
            src_ref=r_out.at[i, side],
            dst_ref=z_in.at[i % NH, (z + NZ - target + NZ - 1) % NZ],
            send_sem=z_send.at[side, i],
            recv_sem=z_recv.at[i % NH],
            device_id=(target * 2 + core, x, y),
            device_id_type=MESH,
        )

    def stage_y1(i):
        c_copy(i).wait_recv()
        for side in range(2):
            s_sum[i, side] = part[i, side, core] + c_in[i, side]
        y1_copy(i, 0).start()
        y1_copy(i, 1).start()

    def stage_y2(i):
        for side in range(2):
            y1_copy(i, side).wait_recv()
            near = up if side == 0 else down
            for u in range(2):
                for half in range(2):
                    lanes = slice(half * HALF, (half + 1) * HALF)
                    value = s_sum[i, u, near, :, lanes]
                    if half == side:
                        value = value + y1_in[i, side, u]
                    y2_out[i, side, u, :, lanes] = value
            y2_copy(i, side).start()

    def stage_z(i):
        y2_copy(i, 0).wait_recv()
        y2_copy(i, 1).wait_recv()
        for u in range(2):
            value = s_sum[i, u, y] + y2_in[i, 0, u] + y2_in[i, 1, u]
            src, zz = piece(i, u)
            target = src * 2 + zz

            @pl.when(target != z)
            def _():
                r_out[i, u] = value
                z_copy(i, u, target).start()

            @pl.when(target == z)
            def _():
                r_own[i % NH] = value

    def compute(i):
        for side in range(2):
            src, zz = piece(i, side)
            for c in range(2):
                flag = a_flags[src * 4 + zz * 2 + c]
                kept = a_all[i, side, c].reshape(4 * SUB, CD) * flag
                hi = kept.astype(jnp.bfloat16)
                lo = (kept - hi.astype(jnp.float32)).astype(jnp.bfloat16)
                at = (side * 2 + c) * 4 * SUB
                a_hl[at : at + 4 * SUB, :] = hi
                a_hl[at + 16 * SUB : at + 20 * SUB, :] = lo

        @pl.loop(0, AB // 256)
        def _(n):
            lanes = pl.ds(pl.multiple_of(n * 256, 256), 256)
            both = jnp.dot(a_hl[...], v_hi[:, lanes], preferred_element_type=jnp.float32)
            low = jnp.dot(
                a_hl[0 : 16 * SUB, :], v_lo[:, lanes], preferred_element_type=jnp.float32
            )
            total = both[0 : 16 * SUB, :] + (both[16 * SUB :, :] + low)
            part[i, :, :, :, :, lanes] = total.reshape(2, 2, 4, SUB, 256)

        c_copy(i).start()

    @pl.loop(0, STEPS + 3)
    def _(i):
        @pl.when((i >= 1) & (i < STEPS + 1))
        def _():
            stage_y1(i - 1)

        @pl.when((i >= 2) & (i < STEPS + 2))
        def _():
            stage_y2(i - 2)

        @pl.when(i >= 3)
        def _():
            stage_z(i - 3)

        @pl.when(i < NH)
        def _():
            own_copy(i, 0).wait()
            own_copy(i, 1).wait()

        @pl.when((i >= NH) & (i < STEPS))
        def _():
            for side in range(2):
                pltpu.make_async_copy(
                    a_all.at[i, side], a_all.at[i, side], a_recv.at[side, i - NH]
                ).wait()

        @pl.when((i >= NH) & (i < 2 * NH))
        def _():
            a_forward(i - NH, 0).start()
            a_forward(i - NH, 1).start()

        @pl.when(i < STEPS)
        def _():
            compute(i)

    for h in range(NH):
        pltpu.make_async_copy(
            z_in.at[h, pl.ds(0, NZ - 1)], z_in.at[h, pl.ds(0, NZ - 1)], z_recv.at[h]
        ).wait()
        total = r_own[h]
        for k in range(NZ - 1):
            total = total + z_in[h, k]
        out[h * SUB : (h + 1) * SUB, :] = total

    for side in range(2):
        @pl.loop(0, 2 * NH)
        def _(j):
            pltpu.make_async_copy(
                a_all.at[NH + j, side], a_all.at[NH + j, side], a_send.at[side, j]
            ).wait()

        @pl.loop(0, NH)
        def _(j):
            a_forward(j, side).wait_send()

    @pl.loop(0, STEPS)
    def _(i):
        c_copy(i).wait_send()
        for side in range(2):
            y1_copy(i, side).wait_send()
            y2_copy(i, side).wait_send()
            src, zz = piece(i, side)
            target = src * 2 + zz

            @pl.when(target != z)
            def _():
                z_copy(i, side, target).wait_send()


def per_device(residual, amplitudes, integrals, t2_mask, v_mask):
    f32, bf16, dma = jnp.float32, jnp.bfloat16, pltpu.SemaphoreType.DMA
    summed = pl.pallas_call(
        kernel,
        out_shape=jax.ShapeDtypeStruct((32, AB), f32),
        in_specs=[pl.BlockSpec(memory_space=pl.ANY)] * 4,
        out_specs=pl.BlockSpec(memory_space=pltpu.VMEM),
        scratch_shapes=[
            pltpu.VMEM((STEPS, 2, 2, 4, SUB, CD), f32),
            pltpu.VMEM((CD, AB), f32),
            pltpu.VMEM((CD, AB), bf16),
            pltpu.VMEM((CD, AB), bf16),
            pltpu.VMEM((32 * SUB, CD), bf16),
            pltpu.VMEM((STEPS, 2, 2, 4, SUB, AB), f32),
            pltpu.VMEM((STEPS, 2, 4, SUB, AB), f32),
            pltpu.VMEM((STEPS, 2, 4, SUB, AB), f32),
            pltpu.VMEM((STEPS, 2, 2, SUB, HALF), f32),
            pltpu.VMEM((STEPS, 2, 2, SUB, AB), f32),
            pltpu.VMEM((STEPS, 2, 2, SUB, AB), f32),
            pltpu.VMEM((STEPS, 2, SUB, AB), f32),
            pltpu.VMEM((NH, SUB, AB), f32),
            pltpu.VMEM((NH, NZ - 1, SUB, AB), f32),
            pltpu.VMEM((NX, 4, 8), jnp.int32),
            pltpu.VMEM((8, 8), jnp.int32),
            pltpu.VMEM((16, 1, CD), f32),
            dma((2, 3 * NH)),
            dma((2, 3 * NH)),
            dma((NH, 2)),
            dma((8,)),
            dma((NX - 1,)),
            dma((NX - 1,)),
            dma((2,)),
            dma((STEPS,)),
            dma((STEPS,)),
            dma((2, STEPS)),
            dma((2, STEPS)),
            dma((2, STEPS)),
            dma((2, STEPS)),
            dma((2, STEPS)),
            dma((NH,)),
        ],
        compiler_params=pltpu.CompilerParams(
            collective_id=0, has_side_effects=True, vmem_limit_bytes=56 * 1024 * 1024
        ),
        name="ladder",
    )(amplitudes.reshape(2, 2, 4, 32, CD), integrals, t2_mask, v_mask)
    return residual + summed


def solution(mesh):
    in_specs = (
        P(("row", "depth"), "col"),
        P("col", ("row", "depth")),
        P(("row", "depth"), "col"),
        P("col", ("row", "depth")),
        P(("row", "depth"), "col"),
    )
    out_specs = P(("row", "depth"), "col")
    return jax.shard_map(
        per_device, mesh=mesh, in_specs=in_specs, out_specs=out_specs, check_vma=False
    )
```

time: 295 us -> 101 us (0.34)
  waiting for transfers between devices: 241 us -> 0 us
  Pallas kernels: 0 us -> 98.8 us
  matrix products: 32 us -> 0 us
  between operations: 13.4 us -> 0.02 us
  other arithmetic: 5.93 us -> 1.58 us
    reduce_scatter x1 -> x0, waiting for transfers between devices: 153 us -> none  [per_device(): lax.psum_scatter(jnp.dot(panels, integral_kept, precision=lax.Precision.H...]
    pallas_call x0 -> x1, Pallas kernels: none -> 98.8 us  [per_device(): pl.pallas_call(kernel, out_shape=jax.ShapeDtypeStruct((32, AB), f32), in_...]
    all_gather x1 -> x0, waiting for transfers between devices: 88.4 us -> none  [per_device(): panels = lax.all_gather(amplitude_kept, 'col', axis=0, tiled=True)]
    dot_general x1 -> x0, matrix products: 32 us -> none  [per_device(): jnp.dot(panels, integral_kept, precision=lax.Precision.HIGHEST, preferred...]
    mul x1 -> x0, other arithmetic: 3.67 us -> none  [apply_flags(): matrix.reshape(tile_rows, TILE, tile_cols, TILE)]
  transfers between devices with their start and end apart: 2 -> 0, of which waited for: 2 -> 0; matrix products, arithmetic and copies ran while one was open for 0% -> 0% of each run, Pallas kernels for 0% -> 0%
where the time goes in v1:
time: 101 us; the launch traced here: 100 us
  Pallas kernels  98.8 us (98%)
  other arithmetic  1.58 us (2%)
    pallas_call x1, Pallas kernels, per_device(): pl.pallas_call(kernel, out_shape=jax.ShapeDtypeStruct((32, AB), f32), in_...  98.8 us

profile of v1, /device:TPU:4, one launch (start us, length us, event | category | flops | bytes accessed | tf_op | source)
XLA Modules:
  0.0 100.4 jit_solution(11672355240004514488)
XLA Ops:
  0.0 0.0 copy-start
  0.0 98.8 %ladder.1 = f32[32,1024]{1,0:T(8,128)} custom-call(f32[2,2,4,32,1024]{4,3,2,1,0:T(8,128)} %bitcast.1, f32[1024,1024]{1,0:T(8,128)} %integ.1, s32[4,8]{1,0:T(4,128)} %t2_mask.1, s32[8,8]{1,0:T(8,128)} %v_mask.1), custom_call_target="tpu_custom_call" | custom-call | tf_op jit(solution)/shard_map/ladder/pallas_call | solution.py:311
  98.9 0.0 copy-done
  98.9 1.6 %add.3 = f32[32,1024]{1,0:T(8,128)} add(f32[32,1024]{1,0:T(8,128)S(1)} %copy-done, f32[32,1024]{1,0:T(8,128)} %ladder.1) | non-fusion elementwise | flops 32768 | bytes 393216 | tf_op jit(solution)/shard_map/add | solution.py:355
Async XLA Ops:
  0.0 98.9 %copy-start = (f32[32,1024]{1,0:T(8,128)S(1)}, f32[32,1024]{1,0:T(8,128)}, u32[]{:S(2)}) copy-start(f32[32,1024]{1,0:T(8,128)} %param.5) | copy-start | bytes 393220

commit v2 on v0

v2 whole, which is shorter than its diff:
```python
import jax
import jax.numpy as jnp
from jax import lax
from jax.experimental import pallas as pl
from jax.experimental.pallas import tpu as pltpu
from jax.sharding import PartitionSpec as P

TILE = 128
NX, NY, NZ = 4, 4, 8
SUB = 8
NH = 32 // SUB
NJ = 3 * NH
STEPS = NH + NJ
CD = 1024
AB = 1024
HALF = AB // 2
ROWS = 16 * SUB
MESH = pl.DeviceIdType.MESH

EARLY = 2
FWD = NH + EARLY


def expand_lanes(flags):
    values = flags.astype(jnp.float32)
    return jnp.concatenate(
        [jnp.broadcast_to(values[:, q : q + 1], (values.shape[0], TILE)) for q in range(8)],
        axis=1,
    )


def kernel(
    amp, integ, t2_mask, v_mask, out,
    a_all, v_f32, v_hi, v_lo, a_hl, part, c_in, s_sum, far_in, side_in, main_out, main_in,
    r_out, r_own, z_in, t2_all, v_flags, a_flags,
    a_send, a_recv, own_sem, v_sem, m_send, m_recv, m_sem, c_send, c_recv,
    far_send, far_recv, side_send, side_recv, main_send, main_recv, z_send, z_recv, z_known,
):
    row = lax.axis_index("row")
    x = lax.axis_index("col")
    y = lax.axis_index("depth")
    z = row // 2
    core = row % 2
    right, left = (x + 1) % NX, (x + 3) % NX
    up, down, far = (y + 1) % NY, (y + 3) % NY, (y + 2) % NY
    sibling = z * 2 + 1 - core
    z_next = ((z + 1) % NZ) * 2 + core
    z_prev = ((z + NZ - 1) % NZ) * 2 + core

    barrier = pltpu.get_barrier_semaphore()

    def greet(r, c, d):
        pl.semaphore_signal(barrier, inc=1, device_id=(r, c, d), device_id_type=MESH)

    greet(row, left, y)
    greet(row, right, y)
    greet(sibling, x, y)
    greet(row, x, up)
    greet(row, x, down)
    greet(z_next, x, y)
    greet(z_prev, x, y)

    def own_copy(h, zz):
        return pltpu.make_async_copy(
            amp.at[zz, :, :, pl.ds(h * SUB, SUB), :], a_all.at[h, zz], own_sem.at[h, zz]
        )

    def v_copy(q):
        block = pl.ds(q * TILE, TILE)
        return pltpu.make_async_copy(integ.at[block, :], v_f32.at[block, :], v_sem.at[q])

    m_copy = pltpu.make_async_copy(t2_mask, t2_all.at[x], m_sem.at[0])
    vm_copy = pltpu.make_async_copy(v_mask, v_flags, m_sem.at[1])
    vm_copy.start()
    for q in range(8):
        v_copy(q).start()
    m_copy.start()
    pl.semaphore_wait(barrier, 7)

    def a_own_send(j, zz, h, side):
        return pltpu.make_async_remote_copy(
            src_ref=amp.at[zz, :, :, pl.ds(h * SUB, SUB), :],
            dst_ref=a_all.at[NH + j, side],
            send_sem=a_send,
            recv_sem=a_recv.at[side, j],
            device_id=(row, right if side == 0 else left, y),
            device_id_type=MESH,
        )

    def a_forward(j, side):
        return pltpu.make_async_remote_copy(
            src_ref=a_all.at[NH + j, side],
            dst_ref=a_all.at[NH + FWD + j, side],
            send_sem=a_send,
            recv_sem=a_recv.at[side, FWD + j],
            device_id=(row, right if side == 0 else left, y),
            device_id_type=MESH,
        )

    def flag_send(src, who, k):
        return pltpu.make_async_remote_copy(
            src_ref=src,
            dst_ref=t2_all.at[who],
            send_sem=m_send.at[k],
            recv_sem=m_recv.at[k],
            device_id=(row, left if k == 1 else right, y),
            device_id_type=MESH,
        )

    for j in range(NH):
        for side in range(2):
            a_own_send(j, side, j, side).start()
    flag_send(t2_mask, x, 0).start()
    flag_send(t2_mask, x, 1).start()
    for j in range(EARLY):
        for side in range(2):
            a_own_send(NH + j, 1 - side, j, side).start()
    for h in range(NH):
        own_copy(h, 0).start()
        own_copy(h, 1).start()

    vm_copy.wait()
    flags_v = expand_lanes(v_flags[...])
    for q in range(8):
        v_copy(q).wait()
        rows = slice(q * TILE, (q + 1) * TILE)
        kept = v_f32[rows, :] * flags_v[q : q + 1, :]
        hi = kept.astype(jnp.bfloat16)
        v_hi[rows, :] = hi
        v_lo[rows, :] = (kept - hi.astype(jnp.float32)).astype(jnp.bfloat16)

    def widen(s):
        wide = expand_lanes(t2_all[s])
        for p in range(4):
            a_flags[s * 4 + p] = wide[p : p + 1, :]

    m_copy.wait()
    widen(x)

    def piece(i, side):
        second = ((i >= 2 * NH) & (i < 2 * NH + EARLY)) | (i >= 3 * NH + EARLY)
        forwarded = (i >= NH + FWD) & (i < 2 * NH + FWD)
        away = jnp.where(i < NH, 0, jnp.where(forwarded, 2, 1))
        zz = jnp.where(second, 1 - side, side)
        h = jnp.where(forwarded, i - NH - FWD, jnp.where(i >= 3 * NH + EARLY, i - 3 * NH, i % NH))
        src = (x + NX - away) % NX if side == 0 else (x + away) % NX
        return src, zz, h

    def c_copy(i, n):
        return pltpu.make_async_remote_copy(
            src_ref=part.at[i, n, :, 1 - core],
            dst_ref=c_in.at[i, n],
            send_sem=c_send,
            recv_sem=c_recv.at[n, i],
            device_id=(sibling, x, y),
            device_id_type=MESH,
        )

    def main_y(n):
        return up if n == 0 else down

    def side_y(n):
        return down if n == 0 else up

    def far_copy(i, n):
        return pltpu.make_async_remote_copy(
            src_ref=s_sum.at[i, n, far],
            dst_ref=far_in.at[i, n],
            send_sem=far_send,
            recv_sem=far_recv.at[n, i],
            device_id=(row, x, main_y(n)),
            device_id_type=MESH,
        )

    def side_copy(i, n):
        return pltpu.make_async_remote_copy(
            src_ref=s_sum.at[i, n, side_y(n)],
            dst_ref=side_in.at[i, n],
            send_sem=side_send,
            recv_sem=side_recv.at[n, i],
            device_id=(row, x, side_y(n)),
            device_id_type=MESH,
        )

    def main_copy(i, n):
        return pltpu.make_async_remote_copy(
            src_ref=main_out.at[i, n],
            dst_ref=main_in.at[i, n],
            send_sem=main_send,
            recv_sem=main_recv.at[n, i],
            device_id=(row, x, main_y(n)),
            device_id_type=MESH,
        )

    def z_copy(i, n, u, h, target):
        return pltpu.make_async_remote_copy(
            src_ref=r_out.at[i, n, u],
            dst_ref=z_in.at[h, n, (z + NZ - target + NZ - 1) % NZ],
            send_sem=z_send,
            recv_sem=z_recv.at[n, h],
            device_id=(target * 2 + core, x, y),
            device_id_type=MESH,
        )

    def stage_far(i, n):
        c_copy(i, n).wait_recv()
        for u in range(2):
            s_sum[i, n, :, u] = part[i, n, u, core] + c_in[i, n, u]
        far_copy(i, n).start()
        side_copy(i, n).start()

    def stage_main(i, n):
        far_copy(i, n).wait_recv()
        main_out[i, n] = s_sum[i, n, main_y(n)] + far_in[i, n]
        main_copy(i, n).start()

    def stage_z(i, n):
        side_copy(i, n).wait_recv()
        main_copy(i, n).wait_recv()
        value = s_sum[i, n, y] + side_in[i, n] + main_in[i, n]
        for u in range(2):
            src, zz, h = piece(i, u)
            target = src * 2 + zz

            @pl.when(target != z)
            def _():
                r_out[i, n, u] = value[u]
                z_copy(i, n, u, h, target).start()

            @pl.when(target == z)
            def _():
                r_own[h, n] = value[u]

    def compute(i):
        for side in range(2):
            src, zz, _ = piece(i, side)
            for c in range(2):
                flag = a_flags[src * 4 + zz * 2 + c]
                kept = a_all[i, side, c].reshape(4 * SUB, CD) * flag
                hi = kept.astype(jnp.bfloat16)
                lo = (kept - hi.astype(jnp.float32)).astype(jnp.bfloat16)
                at = (side * 2 + c) * 4 * SUB
                a_hl[at : at + 4 * SUB, :] = hi
                a_hl[at + ROWS : at + ROWS + 4 * SUB, :] = lo
        for n in range(2):
            for m in range(2):
                at = n * HALF + m * 256
                lanes = slice(at, at + 256)
                both = jnp.dot(a_hl[...], v_hi[:, lanes], preferred_element_type=jnp.float32)
                low = jnp.dot(
                    a_hl[0:ROWS, :], v_lo[:, lanes], preferred_element_type=jnp.float32
                )
                total = both[0:ROWS, :] + (both[ROWS:, :] + low)
                part[i, n, :, :, :, :, m * 256 : m * 256 + 256] = total.reshape(2, 2, 4, SUB, 256)
            c_copy(i, n).start()

    def know(r):
        pl.semaphore_signal(
            z_known.at[r, 0], inc=1, device_id=(z_next, x, y), device_id_type=MESH
        )
        pl.semaphore_signal(
            z_known.at[r, 1], inc=1, device_id=(z_prev, x, y), device_id_type=MESH
        )

    def known(r):
        pl.semaphore_wait(z_known.at[r, 0], 1)
        pl.semaphore_wait(z_known.at[r, 1], 1)

    @pl.loop(0, STEPS)
    def _(i):
        @pl.when(i < 3)
        def _():
            know(i)

        @pl.when(i >= 1)
        def _():
            stage_far(i - 1, 1)

        @pl.when(i >= 2)
        def _():
            stage_main(i - 2, 1)

        @pl.when(i >= 3)
        def _():
            stage_z(i - 3, 1)

        @pl.when(i < NH)
        def _():
            own_copy(i, 0).wait()
            own_copy(i, 1).wait()

        @pl.when(i == NH)
        def _():
            flag_send(t2_mask, x, 0).wait_recv()
            flag_send(t2_mask, x, 1).wait_recv()
            flag_send(t2_all.at[left], left, 2).start()
            widen(left)
            widen(right)

        @pl.when(i == NH + FWD)
        def _():
            flag_send(t2_all.at[left], left, 2).wait_recv()
            widen((x + 2) % NX)

        @pl.when(i >= NH)
        def _():
            for side in range(2):
                pltpu.make_async_copy(
                    a_all.at[i, side], a_all.at[i, side], a_recv.at[side, i - NH]
                ).wait()

        @pl.when((i >= NH) & (i < 2 * NH))
        def _():
            a_forward(i - NH, 0).start()
            a_forward(i - NH, 1).start()

        @pl.when(i == 2 * NH - 1)
        def _():
            for h in range(EARLY, NH):
                for side in range(2):
                    a_own_send(2 * NH + h, 1 - side, h, side).start()

        compute(i)

        @pl.when(i < 3)
        def _():
            known(i)

        stage_far(i, 0)

        @pl.when(i >= 1)
        def _():
            stage_main(i - 1, 0)

        @pl.when(i >= 2)
        def _():
            stage_z(i - 2, 0)

    last = STEPS - 1
    stage_main(last - 1, 1)
    stage_z(last - 2, 1)
    stage_far(last, 1)
    stage_z(last - 1, 0)
    stage_main(last, 0)
    stage_z(last - 1, 1)
    stage_main(last, 1)
    stage_z(last, 0)
    stage_z(last, 1)

    def all_of(ref, sem):
        pltpu.make_async_copy(ref, ref, sem).wait()

    all_of(a_all.at[pl.ds(NH, NJ)], a_send)
    all_of(c_in, c_send)
    all_of(far_in, far_send)
    all_of(side_in, side_send)
    all_of(main_in, main_send)
    all_of(z_in, z_send)
    for k in range(3):
        flag_send(t2_mask, x, k).wait_send()

    for h in range(NH):
        for n in range(2):
            all_of(z_in.at[h, n], z_recv.at[n, h])
            total = r_own[h, n]
            for k in range(NZ - 1):
                total = total + z_in[h, n, k]
            out[h * SUB : (h + 1) * SUB, n * HALF : (n + 1) * HALF] = total


def per_device(residual, amplitudes, integrals, t2_mask, v_mask):
    f32, bf16, dma = jnp.float32, jnp.bfloat16, pltpu.SemaphoreType.DMA
    summed = pl.pallas_call(
        kernel,
        out_shape=jax.ShapeDtypeStruct((32, AB), f32),
        in_specs=[pl.BlockSpec(memory_space=pl.ANY)] * 4,
        out_specs=pl.BlockSpec(memory_space=pltpu.VMEM),
        scratch_shapes=[
            pltpu.VMEM((STEPS, 2, 2, 4, SUB, CD), f32),
            pltpu.VMEM((CD, AB), f32),
            pltpu.VMEM((CD, AB), bf16),
            pltpu.VMEM((CD, AB), bf16),
            pltpu.VMEM((2 * ROWS, CD), bf16),
            pltpu.VMEM((STEPS, 2, 2, 2, 4, SUB, HALF), f32),
            pltpu.VMEM((STEPS, 2, 2, 4, SUB, HALF), f32),
            pltpu.VMEM((STEPS, 2, 4, 2, SUB, HALF), f32),
            pltpu.VMEM((STEPS, 2, 2, SUB, HALF), f32),
            pltpu.VMEM((STEPS, 2, 2, SUB, HALF), f32),
            pltpu.VMEM((STEPS, 2, 2, SUB, HALF), f32),
            pltpu.VMEM((STEPS, 2, 2, SUB, HALF), f32),
            pltpu.VMEM((STEPS, 2, 2, SUB, HALF), f32),
            pltpu.VMEM((NH, 2, SUB, HALF), f32),
            pltpu.VMEM((NH, 2, NZ - 1, SUB, HALF), f32),
            pltpu.VMEM((NX, 4, 8), jnp.int32),
            pltpu.VMEM((8, 8), jnp.int32),
            pltpu.VMEM((16, 1, CD), f32),
            dma(()),
            dma((2, NJ)),
            dma((NH, 2)),
            dma((8,)),
            dma((3,)),
            dma((3,)),
            dma((2,)),
            dma(()),
            dma((2, STEPS)),
            dma(()),
            dma((2, STEPS)),
            dma(()),
            dma((2, STEPS)),
            dma(()),
            dma((2, STEPS)),
            dma(()),
            dma((2, NH)),
            pltpu.SemaphoreType.REGULAR((3, 2)),
        ],
        compiler_params=pltpu.CompilerParams(
            collective_id=0, has_side_effects=True, vmem_limit_bytes=56 * 1024 * 1024
        ),
        name="ladder",
    )(amplitudes.reshape(2, 2, 4, 32, CD), integrals, t2_mask, v_mask)
    return residual + summed


def solution(mesh):
    in_specs = (
        P(("row", "depth"), "col"),
        P("col", ("row", "depth")),
        P(("row", "depth"), "col"),
        P("col", ("row", "depth")),
        P(("row", "depth"), "col"),
    )
    out_specs = P(("row", "depth"), "col")
    return jax.shard_map(
        per_device, mesh=mesh, in_specs=in_specs, out_specs=out_specs, check_vma=False
    )
```

time: 295 us -> 95.7 us (0.32)
  the two profiles are of different devices: /device:TPU:4 before, /device:TPU:6 now
where the time goes in v2:
time: 95.7 us; the launch traced here: 95.6 us
  Pallas kernels  94 us (98%)
  other arithmetic  1.58 us (2%)
    pallas_call x1, Pallas kernels, per_device(): pl.pallas_call(kernel, out_shape=jax.ShapeDtypeStruct((32, AB), f32), in_...  94 us

profile of v2, /device:TPU:6, one launch (start us, length us, event | category | flops | bytes accessed | tf_op | source)
XLA Modules:
  0.0 95.6 jit_solution(16745152961531561192)
XLA Ops:
  0.0 0.0 copy-start
  0.0 94.0 %ladder.1 = f32[32,1024]{1,0:T(8,128)} custom-call(f32[2,2,4,32,1024]{4,3,2,1,0:T(8,128)} %bitcast.1, f32[1024,1024]{1,0:T(8,128)} %integ.1, s32[4,8]{1,0:T(4,128)} %t2_mask.1, s32[8,8]{1,0:T(8,128)} %v_mask.1), custom_call_target="tpu_custom_call" | custom-call | tf_op jit(solution)/shard_map/ladder/pallas_call | solution.py:373
  94.0 0.0 copy-done
  94.0 1.6 %add.3 = f32[32,1024]{1,0:T(8,128)} add(f32[32,1024]{1,0:T(8,128)S(1)} %copy-done, f32[32,1024]{1,0:T(8,128)} %ladder.1) | non-fusion elementwise | flops 32768 | bytes 393216 | tf_op jit(solution)/shard_map/add | solution.py:421
Async XLA Ops:
  0.0 94.0 %copy-start = (f32[32,1024]{1,0:T(8,128)S(1)}, f32[32,1024]{1,0:T(8,128)}, u32[]{:S(2)}) copy-start(f32[32,1024]{1,0:T(8,128)} %param.5) | copy-start | bytes 393220

commit v3 on v0

v3 whole, which is shorter than its diff:
```python
import jax
import jax.numpy as jnp
from jax import lax
from jax.experimental import pallas as pl
from jax.experimental.pallas import tpu as pltpu
from jax.sharding import PartitionSpec as P

TILE = 128
NX, NY, NZ = 4, 4, 8
SUB = 16
NQ = 32 // SUB
NK = NY * NQ
NJ = 3 * NK
STEPS = NK + NJ
CD = 1024
AB = 1024
HALF = AB // 2
ROWS = 4 * SUB
MESH = pl.DeviceIdType.MESH
LAG = 1
LATE = 28


def expand_lanes(flags):
    values = flags.astype(jnp.float32)
    return jnp.concatenate(
        [jnp.broadcast_to(values[:, q : q + 1], (values.shape[0], TILE)) for q in range(8)],
        axis=1,
    )


def kernel(
    amp, integ, t2_mask, v_mask, out,
    a_all, v_f32, v_hi, v_lo, a_hl, part, c_in, s_out, far_in, near_in,
    r_own, z_in, t2_all, v_flags, a_flags,
    a_send, a_recv, own_sem, v_sem, m_send, m_recv, m_sem, c_send, c_recv,
    far_send, far_recv, near_send, near_recv, z_send, z_recv, z_known,
):
    row = lax.axis_index("row")
    x = lax.axis_index("col")
    y = lax.axis_index("depth")
    z = row // 2
    core = row % 2
    right, left = (x + 1) % NX, (x + 3) % NX
    up, down = (y + 1) % NY, (y + 3) % NY
    sibling = z * 2 + 1 - core
    z_next = ((z + 1) % NZ) * 2 + core
    z_prev = ((z + NZ - 1) % NZ) * 2 + core

    barrier = pltpu.get_barrier_semaphore()

    def greet(r, c, d):
        pl.semaphore_signal(barrier, inc=1, device_id=(r, c, d), device_id_type=MESH)

    greet(row, left, y)
    greet(row, right, y)
    greet(sibling, x, y)
    greet(row, x, up)
    greet(row, x, down)
    greet(z_next, x, y)
    greet(z_prev, x, y)

    def rows_of(k, side):
        middle = (k >= NQ) & (k < 3 * NQ)
        turn = (k + NQ + side) % 2
        kind = jnp.where(k < NQ, 0, jnp.where(middle, 1 + turn, 3))
        owner = (y + jnp.where(k < NQ, 2, jnp.where(middle, 1 + 2 * turn, 0))) % NY
        part_of = jnp.where(middle, (k + NQ) // 2 % NQ, k % NQ)
        return kind, owner, part_of

    block = z // 2
    turn_in = (x + NX - 1 - block) % NX, (x + 1 + NX - block) % NX
    turn_out = (x + NX - block) % NX
    f_last = (
        (turn_in[0] == 1) | (turn_in[0] == 2),
        (turn_in[1] == 3) | (turn_in[1] == 2),
    )
    f_last_out = (turn_out == 1) | (turn_out == 2), (turn_out == 3) | (turn_out == 2)

    def b_slot(k, side):
        late = 0 if k < NK // 2 else jnp.where(f_last_out[side], 0, NK)
        return NK + k + late

    def f_slot(k, side):
        return k + jnp.where(f_last_out[side], 2 * NK, NK + NK // 2)

    def piece(t, side):
        j = t - NK
        split_b = jnp.where(j < NK + NK // 2, 2, jnp.where(j < 2 * NK + NK // 2, 3, 2))
        split_k = jnp.where(
            j < NK + NK // 2, j - NK, jnp.where(j < 2 * NK + NK // 2, j - NK - NK // 2, j - 2 * NK)
        )
        whole_b = jnp.where(j < 2 * NK, 2, 3)
        whole_k = jnp.where(j < 2 * NK, j - NK, j - 2 * NK)
        later_g = jnp.where(f_last[side], whole_b, split_b)
        later_k = jnp.where(f_last[side], whole_k, split_k)
        g = jnp.where(t < NK, 0, jnp.where(j < NK, 1, later_g))
        k = jnp.where(t < NK, t, jnp.where(j < NK, j, later_k))
        away = jnp.where(g == 0, 0, jnp.where(g == 3, 2, 1))
        zz = jnp.where(g == 2, 1 - side, side)
        src = (x + NX - away) % NX if side == 0 else (x + away) % NX
        return src, zz, g, k

    def own_copy(k, zz):
        _, owner, half = rows_of(k, zz)
        return pltpu.make_async_copy(
            amp.at[zz, :, owner, half], a_all.at[k, zz], own_sem.at[zz, k]
        )

    def v_copy(q):
        at = pl.ds(q * TILE, TILE)
        return pltpu.make_async_copy(integ.at[at, :], v_f32.at[at, :], v_sem.at[q])

    m_copy = pltpu.make_async_copy(t2_mask, t2_all.at[x], m_sem.at[0])
    vm_copy = pltpu.make_async_copy(v_mask, v_flags, m_sem.at[1])
    vm_copy.start()
    for q in range(8):
        v_copy(q).start()
    m_copy.start()
    pl.semaphore_wait(barrier, 7)

    def a_own_send(slot, zz, k, side):
        _, owner, half = rows_of(k, side)
        return pltpu.make_async_remote_copy(
            src_ref=amp.at[zz, :, owner, half],
            dst_ref=a_all.at[NK + slot, side],
            send_sem=a_send,
            recv_sem=a_recv.at[side, slot],
            device_id=(row, right if side == 0 else left, y),
            device_id_type=MESH,
        )

    def a_forward(k, side):
        slot = f_slot(k, side)
        return pltpu.make_async_remote_copy(
            src_ref=a_all.at[NK + k, side],
            dst_ref=a_all.at[NK + slot, side],
            send_sem=a_send,
            recv_sem=a_recv.at[side, slot],
            device_id=(row, right if side == 0 else left, y),
            device_id_type=MESH,
        )

    def flag_send(src, who, k):
        return pltpu.make_async_remote_copy(
            src_ref=src,
            dst_ref=t2_all.at[who],
            send_sem=m_send.at[k],
            recv_sem=m_recv.at[k],
            device_id=(row, left if k == 1 else right, y),
            device_id_type=MESH,
        )

    for k in range(NK):
        for side in range(2):
            a_own_send(k, side, k, side).start()
    flag_send(t2_mask, x, 0).start()
    flag_send(t2_mask, x, 1).start()
    for k in range(NK):
        own_copy(k, 0).start()
        own_copy(k, 1).start()
    for k in range(NK // 2):
        for side in range(2):
            a_own_send(b_slot(k, side), 1 - side, k, side).start()
    for side in range(2):
        @pl.when(f_last_out[side])
        def _():
            for k in range(NK // 2, NK):
                a_own_send(b_slot(k, side), 1 - side, k, side).start()

    vm_copy.wait()
    flags_v = expand_lanes(v_flags[...])
    for q in range(8):
        v_copy(q).wait()
        rows = slice(q * TILE, (q + 1) * TILE)
        kept = v_f32[rows, :] * flags_v[q : q + 1, :]
        hi = kept.astype(jnp.bfloat16)
        v_hi[rows, :] = hi
        v_lo[rows, :] = (kept - hi.astype(jnp.float32)).astype(jnp.bfloat16)

    def widen(s):
        wide = expand_lanes(t2_all[s])
        for p in range(4):
            a_flags[s * 4 + p] = wide[p : p + 1, :]

    m_copy.wait()
    widen(x)

    def c_copy(t):
        return pltpu.make_async_remote_copy(
            src_ref=part.at[t, :, 1 - core],
            dst_ref=c_in.at[t],
            send_sem=c_send,
            recv_sem=c_recv.at[t],
            device_id=(sibling, x, y),
            device_id_type=MESH,
        )

    def far_copy(t, u, g, half, way):
        return pltpu.make_async_remote_copy(
            src_ref=s_out.at[t, u, :, pl.ds(way * HALF, HALF)],
            dst_ref=far_in.at[g, u, half, way],
            send_sem=far_send,
            recv_sem=far_recv.at[g, u * 2 * NQ + half * 2 + way],
            device_id=(row, x, up if way == 0 else down),
            device_id_type=MESH,
        )

    def near_copy(t, u, g, half, way):
        return pltpu.make_async_remote_copy(
            src_ref=s_out.at[t, u],
            dst_ref=near_in.at[g, u, half, way],
            send_sem=near_send,
            recv_sem=near_recv.at[g, u * 2 * NQ + half * 2 + way],
            device_id=(row, x, up if way == 0 else down),
            device_id_type=MESH,
        )

    def z_copy(t, u, half, target):
        return pltpu.make_async_remote_copy(
            src_ref=s_out.at[t, u],
            dst_ref=z_in.at[half, (z + NZ - target + NZ - 1) % NZ],
            send_sem=z_send,
            recv_sem=z_recv.at[half],
            device_id=(target * 2 + core, x, y),
            device_id_type=MESH,
        )

    def settle(t):
        c_copy(t).wait_recv()
        for u in range(2):
            src, zz, g, k = piece(t, u)
            kind, _, half = rows_of(k, u)

            @pl.when(kind == 0)
            def _():
                s_out[t, u] = part[t, u, core] + c_in[t, u]
                far_copy(t, u, g, half, 0).start()
                far_copy(t, u, g, half, 1).start()

            for way in range(2):
                @pl.when(kind == 1 + way)
                def _():
                    far_copy(t, u, g, half, way).wait_recv()
                    for w in range(2):
                        lanes = slice(w * HALF, (w + 1) * HALF)
                        value = part[t, u, core, :, lanes] + c_in[t, u, :, lanes]
                        if w == way:
                            value = value + far_in[g, u, half, way]
                        s_out[t, u, :, lanes] = value
                    near_copy(t, u, g, half, way).start()

            @pl.when(kind == 3)
            def _():
                near_copy(t, u, g, half, 0).wait_recv()
                near_copy(t, u, g, half, 1).wait_recv()
                value = part[t, u, core] + c_in[t, u]
                value = value + (near_in[g, u, half, 0] + near_in[g, u, half, 1])
                target = src * 2 + zz

                @pl.when(target != z)
                def _():
                    s_out[t, u] = value
                    z_copy(t, u, half, target).start()

                @pl.when(target == z)
                def _():
                    r_own[half] = value

    def compute(t):
        for side in range(2):
            src, zz, _, _ = piece(t, side)
            for c in range(2):
                kept = a_all[t, side, c] * a_flags[src * 4 + zz * 2 + c]
                hi = kept.astype(jnp.bfloat16)
                lo = (kept - hi.astype(jnp.float32)).astype(jnp.bfloat16)
                at = (side * 2 + c) * SUB
                a_hl[at : at + SUB, :] = hi
                a_hl[at + ROWS : at + ROWS + SUB, :] = lo
        for m in range(AB // 256):
            lanes = slice(m * 256, m * 256 + 256)
            both = jnp.dot(a_hl[...], v_hi[:, lanes], preferred_element_type=jnp.float32)
            low = jnp.dot(a_hl[0:ROWS, :], v_lo[:, lanes], preferred_element_type=jnp.float32)
            total = both[0:ROWS, :] + (both[ROWS:, :] + low)
            part[t, :, :, :, lanes] = total.reshape(2, 2, SUB, 256)
        c_copy(t).start()

    def know(r):
        for way, who in ((0, z_next), (1, z_prev)):
            pl.semaphore_signal(
                z_known.at[r, way], inc=1, device_id=(who, x, y), device_id_type=MESH
            )

    def known(r):
        pl.semaphore_wait(z_known.at[r, 0], 1)
        pl.semaphore_wait(z_known.at[r, 1], 1)

    @pl.loop(0, STEPS)
    def _(t):
        for r in range(3):
            @pl.when(t == 2 * r)
            def _():
                if r > 0:
                    known(r - 1)
                know(r)

        @pl.when(t == NK - 2)
        def _():
            known(2)

        @pl.when(t >= LATE)
        def _():
            settle(t - LAG)

        @pl.when(t < NK)
        def _():
            own_copy(t, 0).wait()
            own_copy(t, 1).wait()

        @pl.when(t == NK)
        def _():
            flag_send(t2_mask, x, 0).wait_recv()
            flag_send(t2_mask, x, 1).wait_recv()
            flag_send(t2_all.at[left], left, 2).start()
            widen(left)
            widen(right)

        @pl.when(t == 2 * NK + NK // 2)
        def _():
            flag_send(t2_all.at[left], left, 2).wait_recv()
            widen((x + 2) % NX)

        @pl.when(t >= NK)
        def _():
            for side in range(2):
                pltpu.make_async_copy(
                    a_all.at[t, side], a_all.at[t, side], a_recv.at[side, t - NK]
                ).wait()

        @pl.when((t >= NK) & (t < 2 * NK))
        def _():
            a_forward(t - NK, 0).start()
            a_forward(t - NK, 1).start()

        for side in range(2):
            @pl.when((t == 2 * NK - 1) & jnp.logical_not(f_last_out[side]))
            def _():
                for k in range(NK // 2, NK):
                    a_own_send(b_slot(k, side), 1 - side, k, side).start()

        compute(t)

        @pl.when((t >= LAG) & (t < LATE))
        def _():
            settle(t - LAG)

    for t in range(STEPS - LAG, STEPS):
        settle(t)

    def all_of(ref, sem):
        pltpu.make_async_copy(ref, ref, sem).wait()

    all_of(a_all.at[pl.ds(NK, NJ)], a_send)
    all_of(c_in, c_send)
    all_of(far_in, far_send)
    all_of(near_in, near_send)
    all_of(z_in, z_send)
    for k in range(3):
        flag_send(t2_mask, x, k).wait_send()

    for half in range(NQ):
        all_of(z_in.at[half], z_recv.at[half])
        total = r_own[half]
        for k in range(NZ - 1):
            total = total + z_in[half, k]
        out[half * SUB : (half + 1) * SUB, :] = total


def per_device(residual, amplitudes, integrals, t2_mask, v_mask):
    f32, bf16, dma = jnp.float32, jnp.bfloat16, pltpu.SemaphoreType.DMA
    summed = pl.pallas_call(
        kernel,
        out_shape=jax.ShapeDtypeStruct((32, AB), f32),
        in_specs=[pl.BlockSpec(memory_space=pl.ANY)] * 4,
        out_specs=pl.BlockSpec(memory_space=pltpu.VMEM),
        scratch_shapes=[
            pltpu.VMEM((STEPS, 2, 2, SUB, CD), f32),
            pltpu.VMEM((CD, AB), f32),
            pltpu.VMEM((CD, AB), bf16),
            pltpu.VMEM((CD, AB), bf16),
            pltpu.VMEM((2 * ROWS, CD), bf16),
            pltpu.VMEM((STEPS, 2, 2, SUB, AB), f32),
            pltpu.VMEM((STEPS, 2, SUB, AB), f32),
            pltpu.VMEM((STEPS, 2, SUB, AB), f32),
            pltpu.VMEM((4, 2, NQ, 2, SUB, HALF), f32),
            pltpu.VMEM((4, 2, NQ, 2, SUB, AB), f32),
            pltpu.VMEM((NQ, SUB, AB), f32),
            pltpu.VMEM((NQ, NZ - 1, SUB, AB), f32),
            pltpu.VMEM((NX, 4, 8), jnp.int32),
            pltpu.VMEM((8, 8), jnp.int32),
            pltpu.VMEM((16, 1, CD), f32),
            dma(()),
            dma((2, NJ)),
            dma((2, NK)),
            dma((8,)),
            dma((3,)),
            dma((3,)),
            dma((2,)),
            dma(()),
            dma((STEPS,)),
            dma(()),
            dma((4, 4 * NQ)),
            dma(()),
            dma((4, 4 * NQ)),
            dma(()),
            dma((NQ,)),
            pltpu.SemaphoreType.REGULAR((3, 2)),
        ],
        compiler_params=pltpu.CompilerParams(
            collective_id=0, has_side_effects=True, vmem_limit_bytes=56 * 1024 * 1024
        ),
        name="ladder",
    )(amplitudes.reshape(2, 2, NY, NQ, SUB, CD), integrals, t2_mask, v_mask)
    return residual + summed


def solution(mesh):
    in_specs = (
        P(("row", "depth"), "col"),
        P("col", ("row", "depth")),
        P(("row", "depth"), "col"),
        P("col", ("row", "depth")),
        P(("row", "depth"), "col"),
    )
    out_specs = P(("row", "depth"), "col")
    return jax.shard_map(
        per_device, mesh=mesh, in_specs=in_specs, out_specs=out_specs, check_vma=False
    )
```

time: 295 us -> 89.5 us (0.30)
  waiting for transfers between devices: 241 us -> 0 us
  Pallas kernels: 0 us -> 87.5 us
  matrix products: 32 us -> 0 us
  between operations: 13.4 us -> 0.02 us
  other arithmetic: 5.93 us -> 1.58 us
    reduce_scatter x1 -> x0, waiting for transfers between devices: 153 us -> none  [per_device(): lax.psum_scatter(jnp.dot(panels, integral_kept, precision=lax.Precision.H...]
    all_gather x1 -> x0, waiting for transfers between devices: 88.4 us -> none  [per_device(): panels = lax.all_gather(amplitude_kept, 'col', axis=0, tiled=True)]
    pallas_call x0 -> x1, Pallas kernels: none -> 87.5 us  [per_device(): pl.pallas_call(kernel, out_shape=jax.ShapeDtypeStruct((32, AB), f32), in_...]
    dot_general x1 -> x0, matrix products: 32 us -> none  [per_device(): jnp.dot(panels, integral_kept, precision=lax.Precision.HIGHEST, preferred...]
    mul x1 -> x0, other arithmetic: 3.67 us -> none  [apply_flags(): matrix.reshape(tile_rows, TILE, tile_cols, TILE)]
  transfers between devices with their start and end apart: 2 -> 0, of which waited for: 2 -> 0; matrix products, arithmetic and copies ran while one was open for 0% -> 0% of each run, Pallas kernels for 0% -> 0%
where the time goes in v3:
time: 89.5 us; the launch traced here: 89.1 us
  Pallas kernels  87.5 us (98%)
  other arithmetic  1.58 us (2%)
    pallas_call x1, Pallas kernels, per_device(): pl.pallas_call(kernel, out_shape=jax.ShapeDtypeStruct((32, AB), f32), in_...  87.5 us

profile of v3, /device:TPU:4, one launch (start us, length us, event | category | flops | bytes accessed | tf_op | source)
XLA Modules:
  0.0 89.1 jit_solution(4747288019777816913)
XLA Ops:
  0.0 0.0 copy-start
  0.0 87.5 %ladder.1 = f32[32,1024]{1,0:T(8,128)} custom-call(f32[2,2,4,2,16,1024]{5,4,3,2,1,0:T(8,128)} %bitcast.1, f32[1024,1024]{1,0:T(8,128)} %integ.1, s32[4,8]{1,0:T(4,128)} %t2_mask.1, s32[8,8]{1,0:T(8,128)} %v_mask.1), custom_call_target="tpu_custom_call" | custom-call | tf_op jit(solution)/shard_map/ladder/pallas_call | solution.py:381
  87.6 0.0 copy-done
  87.6 1.6 %add.3 = f32[32,1024]{1,0:T(8,128)} add(f32[32,1024]{1,0:T(8,128)S(1)} %copy-done, f32[32,1024]{1,0:T(8,128)} %ladder.1) | non-fusion elementwise | flops 32768 | bytes 393216 | tf_op jit(solution)/shard_map/add | solution.py:424
Async XLA Ops:
  0.0 87.6 %copy-start = (f32[32,1024]{1,0:T(8,128)S(1)}, f32[32,1024]{1,0:T(8,128)}, u32[]{:S(2)}) copy-start(f32[32,1024]{1,0:T(8,128)} %param.5) | copy-start | bytes 393220

commit v4 on v3

--- a/solution.py
+++ b/solution.py
@@ -19,6 +19,8 @@
 MESH = pl.DeviceIdType.MESH
 LAG = 1
 LATE = 28
+BODY = STEPS - 2
+FINE = SUB // 2
 
 
 def expand_lanes(flags):
@@ -34,7 +36,7 @@
     a_all, v_f32, v_hi, v_lo, a_hl, part, c_in, s_out, far_in, near_in,
     r_own, z_in, t2_all, v_flags, a_flags,
     a_send, a_recv, own_sem, v_sem, m_send, m_recv, m_sem, c_send, c_recv,
-    far_send, far_recv, near_send, near_recv, z_send, z_recv, z_known,
+    far_send, far_recv, near_send, near_recv, z_send, z_recv, z_known, fine_recv, c_fine_recv,
 ):
     row = lax.axis_index("row")
     x = lax.axis_index("col")
@@ -126,6 +128,29 @@
             dst_ref=a_all.at[NK + slot, side],
             send_sem=a_send,
             recv_sem=a_recv.at[side, slot],
+            device_id=(row, right if side == 0 else left, y),
+            device_id_type=MESH,
+        )
+
+    def a_own_fine(zz, k, side, e):
+        _, owner, half = rows_of(k, side)
+        rows = pl.ds(e * FINE, FINE)
+        return pltpu.make_async_remote_copy(
+            src_ref=amp.at[zz, :, owner, half, rows],
+            dst_ref=a_all.at[STEPS - NK + k, side, :, rows],
+            send_sem=a_send,
+            recv_sem=fine_recv.at[side, (k - NK + 2) * 2 + e],
+            device_id=(row, right if side == 0 else left, y),
+            device_id_type=MESH,
+        )
+
+    def a_forward_fine(k, side, e):
+        rows = pl.ds(e * FINE, FINE)
+        return pltpu.make_async_remote_copy(
+            src_ref=a_all.at[NK + k, side, :, rows],
+            dst_ref=a_all.at[STEPS - NK + k, side, :, rows],
+            send_sem=a_send,
+            recv_sem=fine_recv.at[side, (k - NK + 2) * 2 + e],
             device_id=(row, right if side == 0 else left, y),
             device_id_type=MESH,
         )
@@ -295,7 +320,7 @@
         pl.semaphore_wait(z_known.at[r, 0], 1)
         pl.semaphore_wait(z_known.at[r, 1], 1)
 
-    @pl.loop(0, STEPS)
+    @pl.loop(0, BODY)
     def _(t):
         for r in range(3):
             @pl.when(t == 2 * r)
@@ -339,14 +364,26 @@
 
         @pl.when((t >= NK) & (t < 2 * NK))
         def _():
-            a_forward(t - NK, 0).start()
-            a_forward(t - NK, 1).start()
+            for side in range(2):
+                fine = f_last_out[side] & (t >= 2 * NK - 2)
+
+                @pl.when(jnp.logical_not(fine))
+                def _():
+                    a_forward(t - NK, side).start()
+
+                @pl.when(fine)
+                def _():
+                    for e in range(2):
+                        a_forward_fine(t - NK, side, e).start()
 
         for side in range(2):
             @pl.when((t == 2 * NK - 1) & jnp.logical_not(f_last_out[side]))
             def _():
-                for k in range(NK // 2, NK):
+                for k in range(NK // 2, NK - 2):
                     a_own_send(b_slot(k, side), 1 - side, k, side).start()
+                for k in range(NK - 2, NK):
+                    for e in range(2):
+                        a_own_fine(1 - side, k, side, e).start()
 
         compute(t)
 
@@ -354,8 +391,80 @@
         def _():
             settle(t - LAG)
 
-    for t in range(STEPS - LAG, STEPS):
-        settle(t)
+    settle(BODY - 1)
+
+    def c_fine(q):
+        rows = pl.ds(q % 2 * FINE, FINE)
+        return pltpu.make_async_remote_copy(
+            src_ref=part.at[BODY + q // 2, :, 1 - core, rows],
+            dst_ref=c_in.at[BODY + q // 2, :, rows],
+            send_sem=c_send,
+            recv_sem=c_fine_recv.at[q],
+            device_id=(sibling, x, y),
+            device_id_type=MESH,
+        )
+
+    def compute_fine(q):
+        t, rows = BODY + q // 2, slice(q % 2 * FINE, q % 2 * FINE + FINE)
+        kept = []
+        for side in range(2):
+            src, zz, _, _ = piece(t, side)
+            for c in range(2):
+                kept.append(a_all[t, side, c, rows, :] * a_flags[src * 4 + zz * 2 + c])
+        kept = jnp.concatenate(kept, axis=0)
+        hi = kept.astype(jnp.bfloat16)
+        lo = (kept - hi.astype(jnp.float32)).astype(jnp.bfloat16)
+        n = 4 * FINE
+        a_hl[0:n, :] = hi
+        a_hl[n : 2 * n, :] = lo
+        for m in range(AB // 256):
+            lanes = slice(m * 256, m * 256 + 256)
+            both = jnp.dot(a_hl[0 : 2 * n, :], v_hi[:, lanes], preferred_element_type=jnp.float32)
+            low = jnp.dot(a_hl[0:n, :], v_lo[:, lanes], preferred_element_type=jnp.float32)
+            total = both[0:n, :] + (both[n:, :] + low)
+            part[t, :, :, rows, lanes] = total.reshape(2, 2, FINE, 256)
+        c_fine(q).start()
+
+    def settle_fine(q):
+        t, rows = BODY + q // 2, slice(q % 2 * FINE, q % 2 * FINE + FINE)
+        c_fine(q).wait_recv()
+        for u in range(2):
+            src, zz, g, k = piece(t, u)
+            half = q // 2
+            if q % 2 == 0:
+                near_copy(t, u, g, half, 0).wait_recv()
+                near_copy(t, u, g, half, 1).wait_recv()
+            value = part[t, u, core, rows, :] + c_in[t, u, rows, :]
+            value = value + (near_in[g, u, half, 0, rows, :] + near_in[g, u, half, 1, rows, :])
+            target = src * 2 + zz
+
+            @pl.when(target != z)
+            def _():
+                s_out[t, u, rows, :] = value
+                pltpu.make_async_remote_copy(
+                    src_ref=s_out.at[t, u, pl.ds(q % 2 * FINE, FINE)],
+                    dst_ref=z_in.at[
+                        half, (z + NZ - target + NZ - 1) % NZ, pl.ds(q % 2 * FINE, FINE)
+                    ],
+                    send_sem=z_send,
+                    recv_sem=z_recv.at[half],
+                    device_id=(target * 2 + core, x, y),
+                    device_id_type=MESH,
+                ).start()
+
+            @pl.when(target == z)
+            def _():
+                r_own[half, rows, :] = value
+
+    for q in range(4):
+        for side in range(2):
+            rows = pl.ds(q % 2 * FINE, FINE)
+            piece_half = a_all.at[BODY + q // 2, side, :, rows]
+            pltpu.make_async_copy(piece_half, piece_half, fine_recv.at[side, q]).wait()
+        compute_fine(q)
+        if q > 0:
+            settle_fine(q - 1)
+    settle_fine(3)
 
     def all_of(ref, sem):
         pltpu.make_async_copy(ref, ref, sem).wait()
@@ -415,6 +524,8 @@
             dma(()),
             dma((NQ,)),
             pltpu.SemaphoreType.REGULAR((3, 2)),
+            dma((2, 4)),
+            dma((4,)),
         ],
         compiler_params=pltpu.CompilerParams(
             collective_id=0, has_side_effects=True, vmem_limit_bytes=56 * 1024 * 1024

time: 89.5 us -> 89.4 us (level)
  no operation moved by 1% of the time
where the time goes in v4:
time: 89.4 us; the launch traced here: 89.3 us
  Pallas kernels  87.7 us (98%)
  other arithmetic  1.58 us (2%)
    pallas_call x1, Pallas kernels, per_device(): pl.pallas_call(kernel, out_shape=jax.ShapeDtypeStruct((32, AB), f32), in_...  87.7 us

profile of v4, /device:TPU:4, one launch (start us, length us, event | category | flops | bytes accessed | tf_op | source)
XLA Modules:
  0.0 89.3 jit_solution(16677794350102714578)
XLA Ops:
  0.0 0.0 copy-start
  0.0 87.7 %ladder.1 = f32[32,1024]{1,0:T(8,128)} custom-call(f32[2,2,4,2,16,1024]{5,4,3,2,1,0:T(8,128)} %bitcast.1, f32[1024,1024]{1,0:T(8,128)} %integ.1, s32[4,8]{1,0:T(4,128)} %t2_mask.1, s32[8,8]{1,0:T(8,128)} %v_mask.1), custom_call_target="tpu_custom_call" | custom-call | tf_op jit(solution)/shard_map/ladder/pallas_call | solution.py:490
  87.7 0.0 copy-done
  87.7 1.6 %add.3 = f32[32,1024]{1,0:T(8,128)} add(f32[32,1024]{1,0:T(8,128)S(1)} %copy-done, f32[32,1024]{1,0:T(8,128)} %ladder.1) | non-fusion elementwise | flops 32768 | bytes 393216 | tf_op jit(solution)/shard_map/add | solution.py:535
Async XLA Ops:
  0.0 87.7 %copy-start = (f32[32,1024]{1,0:T(8,128)S(1)}, f32[32,1024]{1,0:T(8,128)}, u32[]{:S(2)}) copy-start(f32[32,1024]{1,0:T(8,128)} %param.5) | copy-start | bytes 393220

commit v5 on v4

--- a/solution.py
+++ b/solution.py
@@ -469,6 +469,13 @@
     def all_of(ref, sem):
         pltpu.make_async_copy(ref, ref, sem).wait()
 
+    for half in range(NQ):
+        all_of(z_in.at[half], z_recv.at[half])
+        total = r_own[half]
+        for k in range(NZ - 1):
+            total = total + z_in[half, k]
+        out[half * SUB : (half + 1) * SUB, :] = total
+
     all_of(a_all.at[pl.ds(NK, NJ)], a_send)
     all_of(c_in, c_send)
     all_of(far_in, far_send)
@@ -476,13 +483,6 @@
     all_of(z_in, z_send)
     for k in range(3):
         flag_send(t2_mask, x, k).wait_send()
-
-    for half in range(NQ):
-        all_of(z_in.at[half], z_recv.at[half])
-        total = r_own[half]
-        for k in range(NZ - 1):
-            total = total + z_in[half, k]
-        out[half * SUB : (half + 1) * SUB, :] = total
 
 
 def per_device(residual, amplitudes, integrals, t2_mask, v_mask):

time: 89.4 us -> 89.4 us (level)
  no operation moved by 1% of the time
where the time goes in v5:
time: 89.4 us; the launch traced here: 89.3 us
  Pallas kernels  87.7 us (98%)
  other arithmetic  1.58 us (2%)
    pallas_call x1, Pallas kernels, per_device(): pl.pallas_call(kernel, out_shape=jax.ShapeDtypeStruct((32, AB), f32), in_...  87.7 us

profile of v5, /device:TPU:4, one launch (start us, length us, event | category | flops | bytes accessed | tf_op | source)
XLA Modules:
  0.0 89.3 jit_solution(5423349015406821005)
XLA Ops:
  0.0 0.0 copy-start
  0.0 87.7 %ladder.1 = f32[32,1024]{1,0:T(8,128)} custom-call(f32[2,2,4,2,16,1024]{5,4,3,2,1,0:T(8,128)} %bitcast.1, f32[1024,1024]{1,0:T(8,128)} %integ.1, s32[4,8]{1,0:T(4,128)} %t2_mask.1, s32[8,8]{1,0:T(8,128)} %v_mask.1), custom_call_target="tpu_custom_call" | custom-call | tf_op jit(solution)/shard_map/ladder/pallas_call | solution.py:490
  87.7 0.0 copy-done
  87.7 1.6 %add.3 = f32[32,1024]{1,0:T(8,128)} add(f32[32,1024]{1,0:T(8,128)S(1)} %copy-done, f32[32,1024]{1,0:T(8,128)} %ladder.1) | non-fusion elementwise | flops 32768 | bytes 393216 | tf_op jit(solution)/shard_map/add | solution.py:535
Async XLA Ops:
  0.0 87.7 %copy-start = (f32[32,1024]{1,0:T(8,128)S(1)}, f32[32,1024]{1,0:T(8,128)}, u32[]{:S(2)}) copy-start(f32[32,1024]{1,0:T(8,128)} %param.5) | copy-start | bytes 393220
